TPU v7x, 32 devices: a whole 2x2x4 slice. The times are simulated.
32 devices in a mesh: param: 8 (over y, x, core), ex: 4 (over z).
Axes of the slice: x: 2, y: 2, z: 4, core: 2. Of those that a mesh axis runs over, the one named last changes fastest.
Arguments:
- grads: float32 [49152, 2048], P('param', 'ex'), may hold values from -6 to 6
- projection: bfloat16 [49152, 1024], P('param'), may hold values from -6 to 6
- whitener: float32 [1024, 1024], P('param'), may hold values from -1 to 3
Outputs:
- scores: float32 [2048, 2048], P('ex', 'param')
All inputs are finite; a program needn't handle non-finite values.
Results may differ from a plain program's by a relative error of at most 0.0052.
Values may be sent and summed in bfloat16 or wider, within the bound.
A program may use at most 128 MiB of HBM per device.

v0:
```python
import math

import jax
import jax.numpy as jnp
from jax import lax
from jax.sharding import PartitionSpec as P


def body(grads, projection, whitener):
    low_grads = grads.astype(jnp.bfloat16)
    partial_value = lax.dot_general(
        projection, low_grads, (((0,), (0,)), ((), ())), preferred_element_type=jnp.float32
    )
    param_count = lax.axis_size("param")
    ex_count = lax.axis_size("ex")
    norm_factor = 1.0 / math.sqrt(grads.shape[0] * param_count)
    whole_whitener = lax.all_gather(whitener, "param", axis=0, tiled=True)
    sketch_rows = partial_value.shape[0]
    local_width = grads.shape[1]
    total_width = local_width * ex_count
    tile_width = total_width // param_count
    col_start = lax.axis_index("param") * tile_width
    owned_share = (
        lax.psum_scatter(partial_value, "param", scatter_dimension=1, tiled=True) * norm_factor
    )
    whitened = jnp.dot(whole_whitener, owned_share, precision=lax.Precision.HIGHEST).astype(
        jnp.bfloat16
    )
    joined = lax.all_gather(whitened, ("param", "ex"), axis=1, tiled=True)
    piece_width = owned_share.shape[1]
    all_columns = joined.reshape(sketch_rows, param_count, ex_count, piece_width)
    all_columns = all_columns.transpose(0, 2, 1, 3).reshape(
        sketch_rows, param_count * ex_count * piece_width
    )
    row_start = lax.axis_index("ex") * local_width
    row_block = lax.dynamic_slice_in_dim(all_columns, row_start, local_width, 1)
    col_block = lax.dynamic_slice_in_dim(all_columns, col_start, tile_width, 1)
    tile = lax.dot_general(
        row_block, col_block, (((0,), (0,)), ((), ())), preferred_element_type=jnp.float32
    )
    return tile / sketch_rows


def solution(mesh):
    return jax.shard_map(
        body,
        mesh=mesh,
        in_specs=(P("param", "ex"), P("param", None), P("param", None)),
        out_specs=P("ex", "param"),
        check_vma=False,
    )
```

profile of v0, /device:TPU:3, one launch (start us, length us, event | category | flops | bytes accessed | tf_op | source)
XLA Modules:
  0.0 181.5 jit_solution(3519660130798700273)
XLA Ops:
  6.5 0.0 reduce-scatter.4.cloned.1.call-start
  6.5 14.3 %fusion.2 = f32[512,1024]{1,0:T(8,128)} fusion(bf16[6144,1024]{1,0:T(8,128)(2,1)} %param.4, f32[6144,512]{1,0:T(8,128)} %param.3), kind=kOutput, calls=%fused_computation.2 | convolution fusion | flops 6445596672 | bytes 27262976
  20.9 0.0 reduce-scatter.4.cloned.1.call-update
  20.9 0.0 all-gather.3.cloned.1.call-start
  20.9 0.7 all-gather.3.cloned.1.call-update
  21.6 0.0 all-gather.5.cloned.1.call-start
  21.7 41.5 %reduce-scatter.4.cloned.1.call-done = f32[64,1024]{1,0:T(8,128)} async-done(((f32[512,1024]{1,0:T(8,128)}), f32[64,1024]{1,0:T(8,128)}) %reduce-scatter.4.cloned.1.call-update) | async-done | bytes 262160
  63.2 1.1 copy.9
  64.3 37.9 %all-gather.3.cloned.1.call-done = f32[1024,1024]{1,0:T(8,128)} async-done(((f32[128,1024]{1,0:T(8,128)}), f32[1024,1024]{1,0:T(8,128)}) %all-gather.3.cloned.1.call-update) | async-done | bytes 4194320 | tf_op jit(solution)/shard_map/all_gather | solution.py:17
  102.3 7.2 %fusion.5 = bf16[1024,64]{0,1:T(8,128)(2,1)} fusion(f32[1024,1024]{1,0:T(8,128)} %all-gather.3.cloned.1.call-done, f32[1024,64]{1,0:T(8,128)S(1)} %copy.9), kind=kOutput, calls=%fused_computation.5 | convolution fusion | flops 805437440 | bytes 4587520 | tf_op jit(solution)/shard_map/dot_general | solution.py:26
  109.4 0.0 all-gather.5.cloned.1.call-update
  109.5 61.6 %all-gather.5.cloned.1.call-done = bf16[1024,2048]{0,1:T(8,128)(2,1)} async-done(((bf16[1024,64]{0,1:T(8,128)(2,1)}), bf16[1024,2048]{0,1:T(8,128)(2,1)}) %all-gather.5.cloned.1.call-update) | async-done | bytes 4194320 | tf_op jit(solution)/shard_map/all_gather | solution.py:29
  171.0 2.6 %copy.6 = bf16[1024,8,4,64]{0,3,1,2:T(8,128)(2,1)S(1)} copy(bf16[1024,8,4,64]{0,3,2,1:T(8,128)(2,1)} %bitcast.12) | data formatting | bytes 8388608 | tf_op jit(solution)/shard_map/reshape | solution.py:31
  173.7 1.3 convolution_multiply_fusion
Async XLA Ops:
  6.5 56.7 %reduce-scatter.4.cloned.1.call-start = ((), (), s32[]{:S(2)}) async-start(), calls=%async_computation.3 | async-start | bytes 2359296
  20.9 81.4 %all-gather.3.cloned.1.call-start = ((), (), s32[]{:S(2)}) async-start(), calls=%async_computation.1 | async-start | bytes 4718592 | tf_op jit(solution)/shard_map/all_gather | solution.py:17
  21.6 149.4 %all-gather.5.cloned.1.call-start = ((), (), s32[]{:S(2)}) async-start(), calls=%async_computation.2 | async-start | bytes 4325376 | tf_op jit(solution)/shard_map/all_gather | solution.py:29
Sparse Core Ops, SparseCore 0:
  21.0 42.1 reduce-scatter.3
  65.1 37.1 all-gather.2
  109.6 61.4 all-gather.4
where the time goes:
time: 183 us; the launch traced here: 181 us
  waiting for transfers between devices  142 us (78%)
  matrix products  22.8 us (12%)
  between operations  13.1 us (7%)
  local copies, waits for them, and re-layouts  3.77 us (2%)
    all_gather x1, waiting for transfers between devices, body(): joined = lax.all_gather(whitened, ('param', 'ex'), axis=1, tiled=True)  61.6 us
    unnamed x4, waiting for transfers between devices  42.2 us
    all_gather x1, waiting for transfers between devices, body(): whole_whitener = lax.all_gather(whitener, 'param', axis=0, tiled=True)  37.9 us
    unnamed x1, matrix products  14.3 us
    dot_general x1, matrix products, body(): jnp.dot(whole_whitener, owned_share, precision=lax.Precision.HIGHEST)  7.16 us
  transfers between devices with their start and end apart: 3, of which 3 were waited for; matrix products, arithmetic and copies ran while one was open for 1% of the time, Pallas kernels for 0%

commit v1 on v0

v1 whole, which is shorter than its diff:
```python
import functools
import math

import jax
import jax.numpy as jnp
from jax import lax
from jax.experimental import pallas as pl
from jax.experimental.pallas import tpu as pltpu
from jax.sharding import PartitionSpec as P

MESH = pl.DeviceIdType.MESH
BF16 = jnp.bfloat16
F32 = jnp.float32
N_CHUNKS = 4
K_BLOCK = 512
K_LATER = 1536


def kernel(
    n_p, n_e, norm,
    g_hbm, proj_hbm, w_hbm, out_ref,
    gbuf, pbuf, gt, acc, own, sbuf, rbuf, wf32, wall, wacc, row, zbuf, col,
    g_sem, p0_sem, p_sem, w_sem,
    rs_send, rs_recv, w_send, w_recv, wf_send, wf_recv,
    row_send, row_recv, rf_send, rf_recv, z_send, z_recv, c_send, c_recv, l_sem,
):
    p = lax.axis_index("param")
    e = lax.axis_index("ex")
    depth, width = g_hbm.shape
    sketch = proj_hbm.shape[1]
    jw = sketch // N_CHUNKS
    piece = width // n_p
    wrows = sketch // n_p
    tile = out_ref.shape[1]
    nk = depth // K_BLOCK
    partner = p + 1 - 2 * (p % 2)

    w_load = pltpu.make_async_copy(w_hbm, wf32, w_sem)
    w_load.start()
    g_loads, p0_loads, p_loads = [], [], []
    for k in range(nk):
        rows = pl.ds(k * K_BLOCK, K_BLOCK)
        c = pltpu.make_async_copy(g_hbm.at[rows, :], gbuf.at[rows, :], g_sem.at[k])
        c.start()
        g_loads.append(c)
        c = pltpu.make_async_copy(
            proj_hbm.at[rows, pl.ds(0, jw)], pbuf.at[0, rows, :], p0_sem.at[k]
        )
        c.start()
        p0_loads.append(c)
    for j in range(1, N_CHUNKS):
        c = pltpu.make_async_copy(
            proj_hbm.at[:, pl.ds(j * jw, jw)], pbuf.at[j], p_sem.at[j]
        )
        c.start()
        p_loads.append(c)

    barrier = pltpu.get_barrier_semaphore()
    for d in range(1, n_p):
        pl.semaphore_signal(
            barrier, inc=1, device_id={"param": (p + d) % n_p}, device_id_type=MESH
        )
    for d in range(1, n_e):
        pl.semaphore_signal(
            barrier, inc=1, device_id={"ex": (e + d) % n_e}, device_id_type=MESH
        )
    w_load.wait()
    wall[pl.ds(pl.multiple_of(p * wrows, wrows), wrows), :] = wf32[...].astype(BF16)
    pl.semaphore_wait(barrier, n_p - 1 + n_e - 1)

    def remote(src, dst, ssem, rsem, to):
        return pltpu.make_async_remote_copy(
            src_ref=src, dst_ref=dst, send_sem=ssem, recv_sem=rsem,
            device_id=to, device_id_type=MESH,
        )

    def w_block(q):
        return wall.at[pl.ds(pl.multiple_of(q * wrows, wrows), wrows), :]

    same = [(p + 2 * d) % n_p for d in range(1, n_p // 2)]
    other = [(partner + 2 * d) % n_p for d in range(1, n_p // 2)]
    w_copies = []
    for d, q in enumerate(same):
        c = remote(w_block(p), w_block(p), w_send.at[d], w_recv.at[p], {"param": q})
        c.start()
        w_copies.append(c)
    c = remote(
        w_block(p), w_block(p), w_send.at[n_p // 2 - 1], w_recv.at[p], {"param": partner}
    )
    c.start()
    w_copies.append(c)

    def forward(block, recv, fsend, frecv, q, d):
        remote(block(q), block(q), fsend.at[d], recv.at[q], {"param": partner}).wait_recv()
        c = remote(block(q), block(q), fsend.at[d], frecv.at[q], {"param": partner})
        c.start()
        return c

    rs_copies = []

    def finish_chunk(j):
        cols = pl.ds(j * jw, jw)
        own[:, cols] = acc[pl.ds(pl.multiple_of(p * piece, piece), piece), :]
        sbuf[:, cols] = acc[...].astype(BF16)
        for d in range(1, n_p):
            q = (p + d) % n_p
            c = remote(
                sbuf.at[pl.ds(pl.multiple_of(q * piece, piece), piece), cols],
                rbuf.at[p, :, cols],
                rs_send.at[j, d],
                rs_recv.at[j, p],
                {"param": q},
            )
            c.start()
            rs_copies.append(c)

    def absorb_chunk(j):
        cols = pl.ds(j * jw, jw)
        total = own[:, cols]
        for d in range(1, n_p):
            q = (p + d) % n_p
            remote(
                sbuf.at[pl.ds(0, piece), cols], rbuf.at[q, :, cols],
                rs_send.at[j, d], rs_recv.at[j, q], {"param": q},
            ).wait_recv()
            total = total + rbuf[q, :, cols].astype(F32)
        total = total * norm
        high = total.astype(BF16)
        low = (total - high.astype(F32)).astype(BF16)
        both = jnp.concatenate([high, low], axis=0)
        part = lax.dot_general(
            both, wall[:, cols], (((1,), (1,)), ((), ())), preferred_element_type=F32
        )
        part = part[:piece] + part[piece:]
        if j == 0:
            wacc[...] = part
        else:
            wacc[...] += part

    acc[...] = jnp.zeros_like(acc)
    for k in range(nk):
        g_loads[k].wait()
        p0_loads[k].wait()

        rows = pl.ds(k * K_BLOCK, K_BLOCK)
        gk = gbuf[rows, :].astype(BF16).T
        gt[:, rows] = gk
        acc[...] += jnp.dot(gk, pbuf[0, rows, :], preferred_element_type=F32)
    finish_chunk(0)
    forwards = []
    for j in range(1, N_CHUNKS):
        p_loads[j - 1].wait()
        acc[...] = jnp.zeros_like(acc)

        @pl.loop(0, depth // K_LATER)
        def _(k):
            rows = pl.ds(pl.multiple_of(k * K_LATER, K_LATER), K_LATER)
            acc[...] += jnp.dot(gt[:, rows], pbuf[j, rows, :], preferred_element_type=F32)

        finish_chunk(j)
        if j == 2:
            for d, q in enumerate(same):
                forwards.append(forward(w_block, w_recv, wf_send, wf_recv, q, d))
    remote(
        w_block(p), w_block(partner), w_send.at[0], w_recv.at[partner], {"param": partner}
    ).wait_recv()
    for d, q in enumerate(other):
        remote(
            w_block(q), w_block(q), wf_send.at[d], wf_recv.at[q], {"param": partner}
        ).wait_recv()
    for j in range(N_CHUNKS):
        absorb_chunk(j)

    def row_block(q):
        return row.at[pl.ds(pl.multiple_of(q * piece, piece), piece), :]

    row[pl.ds(pl.multiple_of(p * piece, piece), piece), :] = wacc[...].astype(BF16)
    out_copies = []
    for d in range(1, n_e):
        c = remote(
            row_block(p), zbuf.at[e], z_send.at[d], z_recv.at[e], {"ex": (e + d) % n_e}
        )
        c.start()
        out_copies.append(c)
    for d, q in enumerate(same):
        c = remote(row_block(p), row_block(p), row_send.at[d], row_recv.at[p], {"param": q})
        c.start()
        out_copies.append(c)
    c = remote(
        row_block(p), row_block(p), row_send.at[n_p // 2 - 1], row_recv.at[p],
        {"param": partner},
    )
    c.start()
    out_copies.append(c)

    def pass_on(src, group, d):
        first = group * width + p * piece
        q = first // tile
        slot = (first % tile) // piece
        dst = col.at[pl.ds(pl.multiple_of(slot * piece, piece), piece), :]
        c = remote(src, dst, c_send.at[d], c_recv.at[slot], {"param": q})
        l = pltpu.make_async_copy(src, dst, l_sem.at[d])

        @pl.when(q != p)
        def _():
            c.start()

        @pl.when(q == p)
        def _():
            l.start()

        return q, c, l

    passed = [pass_on(row_block(p), e, 0)]
    for d in range(1, n_e):
        s = (e + d) % n_e
        remote(
            row_block(p), zbuf.at[s], z_send.at[d], z_recv.at[s], {"ex": s}
        ).wait_recv()
        passed.append(pass_on(zbuf.at[s], s, d))
    for d, q in enumerate(same):
        forwards.append(forward(row_block, row_recv, rf_send, rf_recv, q, d))
    remote(
        row_block(p), row_block(partner), row_send.at[0], row_recv.at[partner],
        {"param": partner},
    ).wait_recv()
    for d, q in enumerate(other):
        remote(
            row_block(q), row_block(q), rf_send.at[d], rf_recv.at[q], {"param": partner}
        ).wait_recv()
    for q, c, l in passed:

        @pl.when(q == p)
        def _(l=l):
            l.wait()

        @pl.when(q != p)
        def _(c=c):
            c.wait_send()

    for slot in range(tile // piece):
        source = ((p * tile) % width) // piece + slot
        dst = col.at[pl.ds(slot * piece, piece), :]

        @pl.when(source != p)
        def _(slot=slot, dst=dst):
            remote(
                row_block(p), dst, c_send.at[0], c_recv.at[slot], {"param": partner}
            ).wait_recv()

    result = lax.dot_general(
        row[...], col[...], (((1,), (1,)), ((), ())), preferred_element_type=F32
    )
    out_ref[...] = result * (1.0 / sketch)

    for c in w_copies + rs_copies + out_copies + forwards:
        c.wait_send()


def solution(mesh):
    n_p, n_e = mesh.shape["param"], mesh.shape["ex"]

    def body(grads, projection, whitener):
        depth, width = grads.shape
        sketch = projection.shape[1]
        piece = width // n_p
        tile = width * n_e // n_p
        jw = sketch // N_CHUNKS
        nk = depth // K_BLOCK
        dma = pltpu.SemaphoreType.DMA
        norm = 1.0 / math.sqrt(depth * n_p)
        half = n_p // 2
        return pl.pallas_call(
            functools.partial(kernel, n_p, n_e, norm),
            out_shape=jax.ShapeDtypeStruct((width, tile), F32),
            in_specs=[pl.BlockSpec(memory_space=pl.ANY)] * 3,
            out_specs=pl.BlockSpec(memory_space=pltpu.VMEM),
            scratch_shapes=[
                pltpu.VMEM((depth, width), F32),
                pltpu.VMEM((N_CHUNKS, depth, jw), BF16),
                pltpu.VMEM((width, depth), BF16),
                pltpu.VMEM((width, jw), F32),
                pltpu.VMEM((piece, sketch), F32),
                pltpu.VMEM((width, sketch), BF16),
                pltpu.VMEM((n_p, piece, sketch), BF16),
                pltpu.VMEM(whitener.shape, F32),
                pltpu.VMEM((sketch, sketch), BF16),
                pltpu.VMEM((piece, sketch), F32),
                pltpu.VMEM((width, sketch), BF16),
                pltpu.VMEM((n_e, piece, sketch), BF16),
                pltpu.VMEM((tile, sketch), BF16),
                dma((nk,)), dma((nk,)), dma((N_CHUNKS,)), dma,
                dma((N_CHUNKS, n_p)), dma((N_CHUNKS, n_p)),
                dma((half,)), dma((n_p,)), dma((half,)), dma((n_p,)),
                dma((half,)), dma((n_p,)), dma((half,)), dma((n_p,)),
                dma((n_e,)), dma((n_e,)), dma((n_e,)), dma((tile // piece,)), dma((n_e,)),
            ],
            compiler_params=pltpu.CompilerParams(
                collective_id=0, has_side_effects=True, vmem_limit_bytes=67043328
            ),
        )(grads, projection, whitener)

    return jax.shard_map(
        body,
        mesh=mesh,
        in_specs=(P("param", "ex"), P("param", None), P("param", None)),
        out_specs=P("ex", "param"),
        check_vma=False,
    )
```

time: 183 us -> 58.5 us (0.32)
  the two profiles are of different devices: /device:TPU:3 before, /device:TPU:9 now
where the time goes in v1:
time: 58.5 us; the launch traced here: 58.3 us
  Pallas kernels  56.4 us (96%)
  local copies, waits for them, and re-layouts  1.87 us (3%)
    pallas_call x1, Pallas kernels, body(): pl.pallas_call(functools.partial(kernel, n_p, n_e, norm), out_shape=jax.S...  56.4 us
    unnamed x1, local copies, waits for them, and re-layouts  1.87 us

profile of v1, /device:TPU:9, one launch (start us, length us, event | category | flops | bytes accessed | tf_op | source)
XLA Modules:
  0.0 58.3 jit_solution(4274052696425719795)
XLA Ops:
  0.0 56.4 %shard_map.37 = f32[512,256]{1,0:T(8,128)} custom-call(f32[6144,512]{1,0:T(8,128)} %g_hbm.1, bf16[6144,1024]{1,0:T(8,128)(2,1)} %proj_hbm.1, f32[128,1024]{1,0:T(8,128)} %w_hbm.1), custom_call_target="tpu_custom_call" | custom-call | tf_op jit(solution)/shard_map/pallas_call | solution.py:273
  56.4 1.9 %copy.5 = f32[512,256]{1,0:T(8,128)} copy(f32[512,256]{1,0:T(8,128)} %shard_map.37) | data formatting | bytes 1048576

commit v2 on v0

v2 whole, which is shorter than its diff:
```python
import functools
import math

import jax
import jax.numpy as jnp
from jax import lax
from jax.experimental import pallas as pl
from jax.experimental.pallas import tpu as pltpu
from jax.sharding import PartitionSpec as P

MESH = pl.DeviceIdType.MESH
BF16 = jnp.bfloat16
F32 = jnp.float32
HALVES = 2
K_BLOCK = 512
K_LATER = 1536
B_CHUNKS = (256, 256, 256, 256)


def kernel(
    n_p, n_e, norm,
    g_hbm, proj_hbm, w_hbm, out_ref,
    gbuf, pbuf, gt, acc, keep, xsend, xrecv, sbuf, rbuf, wf32, wall, wacc, row, zbuf, col,
    g_sem, p_sem, w_sem,
    x_send, x_recv, rs_send, rs_recv, w_send, w_recv, wf_send, wf_recv,
    row_send, row_recv, rf_send, rf_recv, z_send, z_recv, c_send, c_recv, l_sem,
):
    p = lax.axis_index("param")
    e = lax.axis_index("ex")
    depth, width = g_hbm.shape
    sketch = proj_hbm.shape[1]
    hw = width // HALVES
    piece = hw // n_p
    wrows = sketch // n_p
    tile = out_ref.shape[1]
    nk = depth // K_BLOCK
    chips = n_p // 2
    chip, core = p // 2, p % 2
    partner = p + 1 - 2 * core

    w_load = pltpu.make_async_copy(w_hbm, wf32, w_sem)
    w_load.start()
    g_loads, p_loads = [], []
    for h in range(HALVES):
        for k in range(nk):
            rows = pl.ds(k * K_BLOCK, K_BLOCK)
            c = pltpu.make_async_copy(
                g_hbm.at[rows, pl.ds(h * hw, hw)], gbuf.at[h, rows, :], g_sem.at[h, k]
            )
            c.start()
            g_loads.append(c)
            if h == 0:
                c = pltpu.make_async_copy(
                    proj_hbm.at[rows, :], pbuf.at[rows, :], p_sem.at[k]
                )
                c.start()
                p_loads.append(c)

    barrier = pltpu.get_barrier_semaphore()
    for d in range(1, n_p):
        pl.semaphore_signal(
            barrier, inc=1, device_id={"param": (p + d) % n_p}, device_id_type=MESH
        )
    for d in range(1, n_e):
        pl.semaphore_signal(
            barrier, inc=1, device_id={"ex": (e + d) % n_e}, device_id_type=MESH
        )
    w_load.wait()
    wall[pl.ds(pl.multiple_of(p * wrows, wrows), wrows), :] = wf32[...].astype(BF16)
    pl.semaphore_wait(barrier, n_p - 1 + n_e - 1)

    def remote(src, dst, ssem, rsem, to):
        return pltpu.make_async_remote_copy(
            src_ref=src, dst_ref=dst, send_sem=ssem, recv_sem=rsem,
            device_id=to, device_id_type=MESH,
        )

    started = []

    def send(*args):
        c = remote(*args)
        c.start()
        started.append(c)

    def w_block(q):
        return wall.at[pl.ds(pl.multiple_of(q * wrows, wrows), wrows), :]

    same = [(p + 2 * d) % n_p for d in range(1, chips)]
    other = [(partner + 2 * d) % n_p for d in range(1, chips)]
    for d, q in enumerate(same):
        send(w_block(p), w_block(p), w_send.at[d], w_recv.at[p], {"param": q})
    send(w_block(p), w_block(p), w_send.at[chips - 1], w_recv.at[p], {"param": partner})

    def forward_w():
        for d, q in enumerate(same):
            remote(
                w_block(q), w_block(q), wf_send.at[d], w_recv.at[q], {"param": q}
            ).wait_recv()
            send(w_block(q), w_block(q), wf_send.at[d], wf_recv.at[q], {"param": partner})

    def await_w():
        remote(
            w_block(p), w_block(partner), w_send.at[0], w_recv.at[partner],
            {"param": partner},
        ).wait_recv()
        for d, q in enumerate(other):
            remote(
                w_block(q), w_block(q), wf_send.at[d], wf_recv.at[q], {"param": partner}
            ).wait_recv()

    def exchange(h, i, first, size):
        cols = pl.ds(first, size)
        for c in range(chips):
            rows = pl.ds(c * piece, piece)
            mine = pl.ds(pl.multiple_of((2 * c + core) * piece, piece), piece)
            theirs = pl.ds(pl.multiple_of((2 * c + 1 - core) * piece, piece), piece)
            keep[h, rows, cols] = acc[mine, pl.ds(0, size)]
            xsend[h, rows, cols] = acc[theirs, pl.ds(0, size)]
        send(
            xsend.at[h, :, cols], xrecv.at[h, :, cols], x_send.at[h, i], x_recv.at[h, i],
            {"param": partner},
        )

    def scatter(h, i, first, size):
        cols = pl.ds(first, size)
        remote(
            xsend.at[h, :, cols], xrecv.at[h, :, cols], x_send.at[h, i], x_recv.at[h, i],
            {"param": partner},
        ).wait_recv()
        both = keep[h, :, cols] + xrecv[h, :, cols]
        keep[h, :, cols] = both
        sbuf[h, :, cols] = both.astype(BF16)
        for d in range(1, chips):
            to = (chip + d) % chips
            send(
                sbuf.at[h, pl.ds(pl.multiple_of(to * piece, piece), piece), cols],
                rbuf.at[h, chip, :, cols],
                rs_send.at[h, i, d],
                rs_recv.at[h, i, chip],
                {"param": 2 * to + core},
            )

    def absorb(h, i, first, size):
        cols = pl.ds(first, size)
        total = keep[h, pl.ds(pl.multiple_of(chip * piece, piece), piece), cols]
        for d in range(1, chips):
            a = (chip + d) % chips
            remote(
                sbuf.at[h, pl.ds(0, piece), cols], rbuf.at[h, a, :, cols],
                rs_send.at[h, i, d], rs_recv.at[h, i, a], {"param": 2 * a + core},
            ).wait_recv()
            total = total + rbuf[h, a, :, cols].astype(F32)
        total = total * norm
        high = total.astype(BF16)
        low = (total - high.astype(F32)).astype(BF16)
        stacked = jnp.concatenate([high, low], axis=0)
        part = lax.dot_general(
            stacked, wall[:, cols], (((1,), (1,)), ((), ())), preferred_element_type=F32
        )
        part = part[:piece] + part[piece:]
        if i == 0:
            wacc[h] = part
        else:
            wacc[h] = wacc[h] + part

    def row_block(h, q):
        return row.at[h, pl.ds(pl.multiple_of(q * piece, piece), piece), :]

    def spread(h):
        row[h, pl.ds(pl.multiple_of(p * piece, piece), piece), :] = wacc[h].astype(BF16)
        mine = row_block(h, p)
        for d in range(1, n_e):
            send(mine, zbuf.at[h, e], z_send.at[h, d], z_recv.at[h, e], {"ex": (e + d) % n_e})
        for d, q in enumerate(same):
            send(mine, mine, row_send.at[h, d], row_recv.at[h, p], {"param": q})
        send(mine, mine, row_send.at[h, chips - 1], row_recv.at[h, p], {"param": partner})
        pass_on(h, mine, e, 0)

    passed = []

    def pass_on(h, src, group, d):
        first = group * width + h * hw + p * piece
        q = first // tile
        slot = (first % tile) // piece
        dst = col.at[pl.ds(pl.multiple_of(slot * piece, piece), piece), :]
        c = remote(src, dst, c_send.at[h, d], c_recv.at[slot], {"param": q})
        l = pltpu.make_async_copy(src, dst, l_sem.at[h, d])

        @pl.when(q != p)
        def _():
            c.start()

        @pl.when(q == p)
        def _():
            l.start()

        passed.append((q, c, l))

    def pass_all(h):
        for d in range(1, n_e):
            s = (e + d) % n_e
            remote(
                row_block(h, p), zbuf.at[h, s], z_send.at[h, d], z_recv.at[h, s], {"ex": s}
            ).wait_recv()
            pass_on(h, zbuf.at[h, s], s, d)

    def forward_rows(h):
        for d, q in enumerate(same):
            block = row_block(h, q)
            remote(block, block, rf_send.at[h, d], row_recv.at[h, q], {"param": q}).wait_recv()
            send(block, block, rf_send.at[h, d], rf_recv.at[h, q], {"param": partner})

    def await_rows(h):
        block = row_block(h, partner)
        remote(
            block, block, row_send.at[h, 0], row_recv.at[h, partner], {"param": partner}
        ).wait_recv()
        for d, q in enumerate(other):
            block = row_block(h, q)
            remote(
                block, block, rf_send.at[h, d], rf_recv.at[h, q], {"param": partner}
            ).wait_recv()

    for k in range(nk):
        rows = pl.ds(k * K_BLOCK, K_BLOCK)
        g_loads[k].wait()
        p_loads[k].wait()
        part = jnp.dot(
            gbuf[0, rows, :].astype(BF16).T, pbuf[rows, :], preferred_element_type=F32
        )
        if k == 0:
            acc[...] = part
        else:
            acc[...] += part
    exchange(0, 0, 0, sketch)

    first = 0
    spans = []
    for i, size in enumerate(B_CHUNKS):
        cols = pl.ds(first, size)
        here = pl.ds(0, size)
        if i == 0:
            for k in range(nk):
                rows = pl.ds(k * K_BLOCK, K_BLOCK)
                g_loads[nk + k].wait()
                gk = gbuf[1, rows, :].astype(BF16).T
                gt[:, rows] = gk
                part = jnp.dot(gk, pbuf[rows, cols], preferred_element_type=F32)
                if k == 0:
                    acc[:, here] = part
                else:
                    acc[:, here] += part
        else:
            acc[:, here] = jnp.zeros((hw, size), F32)

            @pl.loop(0, depth // K_LATER)
            def _(k):
                rows = pl.ds(pl.multiple_of(k * K_LATER, K_LATER), K_LATER)
                acc[:, here] += jnp.dot(
                    gt[:, rows], pbuf[rows, cols], preferred_element_type=F32
                )

        exchange(1, i, first, size)
        if i == 0:
            scatter(0, 0, 0, sketch)
            forward_w()
        else:
            scatter(1, i - 1, *spans[-1])
        if i == 2:
            await_w()
            absorb(0, 0, 0, sketch)
            spread(0)
        spans.append((first, size))
        first += size
    last = len(spans) - 1
    scatter(1, last, *spans[last])
    forward_rows(0)
    for i in range(last):
        absorb(1, i, *spans[i])
    pass_all(0)
    absorb(1, last, *spans[last])
    spread(1)
    await_rows(0)
    forward_rows(1)
    pass_all(1)
    for q, c, l in passed:

        @pl.when(q == p)
        def _(l=l):
            l.wait()

        @pl.when(q != p)
        def _(c=c):
            c.wait_send()

    for slot in range(tile // piece):
        source = ((p * tile) % hw) // piece + slot
        dst = col.at[pl.ds(slot * piece, piece), :]

        @pl.when(source % n_p != p)
        def _(slot=slot, dst=dst):
            remote(
                row_block(0, p), dst, c_send.at[0, 0], c_recv.at[slot], {"param": partner}
            ).wait_recv()

    def product(h):
        out_ref[pl.ds(h * hw, hw), :] = lax.dot_general(
            row[h], col[...], (((1,), (1,)), ((), ())), preferred_element_type=F32
        ) * (1.0 / sketch)

    product(0)
    await_rows(1)
    product(1)
    for c in started:
        c.wait_send()


def solution(mesh):
    n_p, n_e = mesh.shape["param"], mesh.shape["ex"]

    def body(grads, projection, whitener):
        depth, width = grads.shape
        sketch = projection.shape[1]
        hw = width // HALVES
        piece = hw // n_p
        tile = width * n_e // n_p
        nk = depth // K_BLOCK
        dma = pltpu.SemaphoreType.DMA
        norm = 1.0 / math.sqrt(depth * n_p)
        chips = n_p // 2
        steps = len(B_CHUNKS)
        return pl.pallas_call(
            functools.partial(kernel, n_p, n_e, norm),
            out_shape=jax.ShapeDtypeStruct((width, tile), F32),
            in_specs=[pl.BlockSpec(memory_space=pl.ANY)] * 3,
            out_specs=pl.BlockSpec(memory_space=pltpu.VMEM),
            scratch_shapes=[
                pltpu.VMEM((HALVES, depth, hw), F32),
                pltpu.VMEM((depth, sketch), BF16),
                pltpu.VMEM((hw, depth), BF16),
                pltpu.VMEM((hw, sketch), F32),
                pltpu.VMEM((HALVES, hw // 2, sketch), F32),
                pltpu.VMEM((HALVES, hw // 2, sketch), F32),
                pltpu.VMEM((HALVES, hw // 2, sketch), F32),
                pltpu.VMEM((HALVES, hw // 2, sketch), BF16),
                pltpu.VMEM((HALVES, chips, piece, sketch), BF16),
                pltpu.VMEM(whitener.shape, F32),
                pltpu.VMEM((sketch, sketch), BF16),
                pltpu.VMEM((HALVES, piece, sketch), F32),
                pltpu.VMEM((HALVES, hw, sketch), BF16),
                pltpu.VMEM((HALVES, n_e, piece, sketch), BF16),
                pltpu.VMEM((tile, sketch), BF16),
                dma((HALVES, nk)), dma((nk,)), dma,
                dma((HALVES, steps)), dma((HALVES, steps)),
                dma((HALVES, steps, chips)), dma((HALVES, steps, chips)),
                dma((chips,)), dma((n_p,)), dma((chips,)), dma((n_p,)),
                dma((HALVES, chips)), dma((HALVES, n_p)),
                dma((HALVES, chips)), dma((HALVES, n_p)),
                dma((HALVES, n_e)), dma((HALVES, n_e)),
                dma((HALVES, n_e)), dma((tile // piece,)), dma((HALVES, n_e)),
            ],
            compiler_params=pltpu.CompilerParams(
                collective_id=0, has_side_effects=True, vmem_limit_bytes=67043328
            ),
        )(grads, projection, whitener)

    return jax.shard_map(
        body,
        mesh=mesh,
        in_specs=(P("param", "ex"), P("param", None), P("param", None)),
        out_specs=P("ex", "param"),
        check_vma=False,
    )
```

time: 183 us -> 53.4 us (0.29)
  the two profiles are of different devices: /device:TPU:3 before, /device:TPU:17 now
where the time goes in v2:
time: 53.4 us; the launch traced here: 53.3 us
  Pallas kernels  51.4 us (96%)
  local copies, waits for them, and re-layouts  1.87 us (4%)
    pallas_call x1, Pallas kernels, body(): pl.pallas_call(functools.partial(kernel, n_p, n_e, norm), out_shape=jax.S...  51.4 us
    unnamed x1, local copies, waits for them, and re-layouts  1.87 us

profile of v2, /device:TPU:17, one launch (start us, length us, event | category | flops | bytes accessed | tf_op | source)
XLA Modules:
  0.0 53.3 jit_solution(6655305627314784711)
XLA Ops:
  0.0 51.4 %shard_map.37 = f32[512,256]{1,0:T(8,128)} custom-call(f32[6144,512]{1,0:T(8,128)} %g_hbm.1, bf16[6144,1024]{1,0:T(8,128)(2,1)} %proj_hbm.1, f32[128,1024]{1,0:T(8,128)} %w_hbm.1), custom_call_target="tpu_custom_call" | custom-call | tf_op jit(solution)/shard_map/pallas_call | solution.py:332
  51.4 1.9 %copy.5 = f32[512,256]{1,0:T(8,128)} copy(f32[512,256]{1,0:T(8,128)} %shard_map.37) | data formatting | bytes 1048576

commit v3 on v2

--- a/solution.py
+++ b/solution.py
@@ -14,6 +14,7 @@
 HALVES = 2
 K_BLOCK = 512
 K_LATER = 1536
+ENTER_AT = 1
 B_CHUNKS = (256, 256, 256, 256)
 
 
@@ -65,10 +66,6 @@
         pl.semaphore_signal(
             barrier, inc=1, device_id={"ex": (e + d) % n_e}, device_id_type=MESH
         )
-    w_load.wait()
-    wall[pl.ds(pl.multiple_of(p * wrows, wrows), wrows), :] = wf32[...].astype(BF16)
-    pl.semaphore_wait(barrier, n_p - 1 + n_e - 1)
-
     def remote(src, dst, ssem, rsem, to):
         return pltpu.make_async_remote_copy(
             src_ref=src, dst_ref=dst, send_sem=ssem, recv_sem=rsem,
@@ -87,9 +84,13 @@
 
     same = [(p + 2 * d) % n_p for d in range(1, chips)]
     other = [(partner + 2 * d) % n_p for d in range(1, chips)]
-    for d, q in enumerate(same):
-        send(w_block(p), w_block(p), w_send.at[d], w_recv.at[p], {"param": q})
-    send(w_block(p), w_block(p), w_send.at[chips - 1], w_recv.at[p], {"param": partner})
+    def enter():
+        w_load.wait()
+        wall[pl.ds(pl.multiple_of(p * wrows, wrows), wrows), :] = wf32[...].astype(BF16)
+        pl.semaphore_wait(barrier, n_p - 1 + n_e - 1)
+        for d, q in enumerate(same):
+            send(w_block(p), w_block(p), w_send.at[d], w_recv.at[p], {"param": q})
+        send(w_block(p), w_block(p), w_send.at[chips - 1], w_recv.at[p], {"param": partner})
 
     def forward_w():
         for d, q in enumerate(same):
@@ -198,7 +199,7 @@
 
     def pass_all(h):
         for d in range(1, n_e):
-            s = (e + d) % n_e
+            s = (e + n_e - d) % n_e
             remote(
                 row_block(h, p), zbuf.at[h, s], z_send.at[h, d], z_recv.at[h, s], {"ex": s}
             ).wait_recv()
@@ -232,6 +233,8 @@
             acc[...] = part
         else:
             acc[...] += part
+        if k == ENTER_AT:
+            enter()
     exchange(0, 0, 0, sketch)
 
     first = 0
@@ -250,6 +253,8 @@
                     acc[:, here] = part
                 else:
                     acc[:, here] += part
+                if k == nk // 2:
+                    scatter(0, 0, 0, sketch)
         else:
             acc[:, here] = jnp.zeros((hw, size), F32)
 
@@ -261,12 +266,11 @@
                 )
 
         exchange(1, i, first, size)
-        if i == 0:
-            scatter(0, 0, 0, sketch)
-            forward_w()
-        else:
+        if i > 0:
             scatter(1, i - 1, *spans[-1])
         if i == 2:
+            forward_w()
+        if i == 3:
             await_w()
             absorb(0, 0, 0, sketch)
             spread(0)
@@ -280,9 +284,9 @@
     pass_all(0)
     absorb(1, last, *spans[last])
     spread(1)
+    pass_all(1)
     await_rows(0)
     forward_rows(1)
-    pass_all(1)
     for q, c, l in passed:
 
         @pl.when(q == p)

time: 53.4 us -> 50.8 us (0.951)
  the two profiles are of different devices: /device:TPU:17 before, /device:TPU:3 now
where the time goes in v3:
time: 50.8 us; the launch traced here: 50.7 us
  Pallas kernels  48.8 us (96%)
  local copies, waits for them, and re-layouts  1.87 us (4%)
    pallas_call x1, Pallas kernels, body(): pl.pallas_call(functools.partial(kernel, n_p, n_e, norm), out_shape=jax.S...  48.8 us
    unnamed x1, local copies, waits for them, and re-layouts  1.87 us

profile of v3, /device:TPU:3, one launch (start us, length us, event | category | flops | bytes accessed | tf_op | source)
XLA Modules:
  0.0 50.7 jit_solution(5925571367966077327)
XLA Ops:
  0.0 48.8 %shard_map.37 = f32[512,256]{1,0:T(8,128)} custom-call(f32[6144,512]{1,0:T(8,128)} %g_hbm.1, bf16[6144,1024]{1,0:T(8,128)(2,1)} %proj_hbm.1, f32[128,1024]{1,0:T(8,128)} %w_hbm.1), custom_call_target="tpu_custom_call" | custom-call | tf_op jit(solution)/shard_map/pallas_call | solution.py:336
  48.8 1.9 %copy.5 = f32[512,256]{1,0:T(8,128)} copy(f32[512,256]{1,0:T(8,128)} %shard_map.37) | data formatting | bytes 1048576

commit v4 on v3

--- a/solution.py
+++ b/solution.py
@@ -14,7 +14,7 @@
 HALVES = 2
 K_BLOCK = 512
 K_LATER = 1536
-ENTER_AT = 1
+ENTER_AT = 0
 B_CHUNKS = (256, 256, 256, 256)
 
 
@@ -278,12 +278,11 @@
         first += size
     last = len(spans) - 1
     scatter(1, last, *spans[last])
+    for i in range(last + 1):
+        absorb(1, i, *spans[i])
+    spread(1)
+    pass_all(0)
     forward_rows(0)
-    for i in range(last):
-        absorb(1, i, *spans[i])
-    pass_all(0)
-    absorb(1, last, *spans[last])
-    spread(1)
     pass_all(1)
     await_rows(0)
     forward_rows(1)

time: 50.8 us -> 51 us (level)
  no operation moved by 1% of the time
where the time goes in v4:
time: 51 us; the launch traced here: 50.8 us
  Pallas kernels  49 us (96%)
  local copies, waits for them, and re-layouts  1.87 us (4%)
    pallas_call x1, Pallas kernels, body(): pl.pallas_call(functools.partial(kernel, n_p, n_e, norm), out_shape=jax.S...  49 us
    unnamed x1, local copies, waits for them, and re-layouts  1.87 us

profile of v4, /device:TPU:3, one launch (start us, length us, event | category | flops | bytes accessed | tf_op | source)
XLA Modules:
  0.0 50.8 jit_solution(3366640229200976330)
XLA Ops:
  0.0 49.0 %shard_map.37 = f32[512,256]{1,0:T(8,128)} custom-call(f32[6144,512]{1,0:T(8,128)} %g_hbm.1, bf16[6144,1024]{1,0:T(8,128)(2,1)} %proj_hbm.1, f32[128,1024]{1,0:T(8,128)} %w_hbm.1), custom_call_target="tpu_custom_call" | custom-call | tf_op jit(solution)/shard_map/pallas_call | solution.py:335
  49.0 1.9 %copy.5 = f32[512,256]{1,0:T(8,128)} copy(f32[512,256]{1,0:T(8,128)} %shard_map.37) | data formatting | bytes 1048576
